TPU v7x, 128 devices: a whole 4x4x4 slice. The times are simulated.
128 devices in a mesh: sec: 8 (over z, core), blk: 16 (over y, x).
Axes of the slice: x: 4, y: 4, z: 4, core: 2. Of those that a mesh axis runs over, the one named last changes fastest.
Arguments:
- wavefunction: bfloat16 [8, 192, 128, 128], P('sec', 'blk')
- left_env: bfloat16 [8, 20, 192, 128, 128], P('sec', None, 'blk')
- right_env: bfloat16 [8, 20, 192, 128, 128], P('sec', None, 'blk')
- row_offset: int32 [8, 12], P('sec'), may hold values from 0 to 15, as said below
- sector_dims: int32 [8, 192, 2], P('sec', 'blk'), may hold values from 64 to 128
- trunc_ranks: int32 [8, 192], P('sec', 'blk'), may hold values from 32 to 128
Outputs:
- state_new: bfloat16 [8, 192, 128, 128], P('sec', 'blk')
- hstate_new: bfloat16 [8, 192, 128, 128], P('sec', 'blk')
- energy: float32 [8], P('sec')
- next_left: bfloat16 [8, 20, 192, 128, 128], P('sec', None, 'blk')
Inputs may be any that keep to these rules, and one draw needn't show every extreme that they name: The sector with up-charge u and down-charge e is stored in slot u of device (e + row_offset[u]) mod 16; in every section the offsets of some two adjacent up-charges differ by 16 / 2 modulo 16.
All inputs are finite; a program needn't handle non-finite values.
Results may differ from a plain program's by a relative error of at most 0.0067.
Values may be sent and summed in bfloat16 or wider, within the bound.
A program may use at most 128 MiB of HBM per device.

v0:
```python
import jax
import jax.numpy as jnp
from jax import lax
from jax.sharding import PartitionSpec as P


def passed_along(value, axis, by):
    length = lax.axis_size(axis)
    pairs = [(i, i + by) for i in range(length) if 0 <= i + by < length]
    return lax.ppermute(value, axis, pairs)


def route_blocks(state, offsets, device, nblk):
    count = state.shape[0]
    up_val = jnp.arange(count, dtype=jnp.int32)
    prev_off = jnp.roll(offsets, 1)
    next_off = jnp.roll(offsets, -1)
    down_val = (device - offsets) % nblk
    exists = [up_val >= 1, up_val <= count - 2, down_val >= 1, down_val <= nblk - 2]
    whole = lax.all_gather(state, "blk", axis=0, tiled=True)
    row_lo = jnp.clip(up_val - 1, 0, count - 1)
    row_hi = jnp.clip(up_val + 1, 0, count - 1)
    indices = [
        (down_val + prev_off) % nblk * count + row_lo,
        (down_val + next_off) % nblk * count + row_hi,
        (device - 1) % nblk * count + up_val,
        (device + 1) % nblk * count + up_val,
    ]
    picked = [jnp.take(whole, entry, axis=0) for entry in indices]
    result = [state]
    for ctype in range(4):
        result.append(
            jnp.where(exists[ctype][:, None, None], picked[ctype], jnp.zeros_like(picked[ctype]))
        )
    return result


def apply_ham(state, lenv, renv, mask, offsets, device, nblk):
    blocks = route_blocks(state, offsets, device, nblk)
    total = jnp.zeros(state.shape, jnp.float32)
    for ctype in range(5):
        inner = jnp.einsum(
            "wtab,tbc->wtac", lenv[ctype::5], blocks[ctype], preferred_element_type=jnp.float32
        ).astype(jnp.bfloat16)
        total = total + jnp.einsum(
            "wtac,wtdc->tad", inner, renv[ctype::5], preferred_element_type=jnp.float32
        )
    return total * mask


def shards(wavefunction, left_env, right_env, row_offset, sector_dims, trunc_ranks):
    start = wavefunction[0]
    lenv = left_env[0]
    renv = right_env[0]
    offsets = row_offset[0]
    dims = sector_dims[0]
    kept_cols = trunc_ranks[0]
    count = start.shape[0]
    width = start.shape[1]
    channels = lenv.shape[0]
    nblk = lax.axis_size("blk")
    device = lax.axis_index("blk")
    cells = float(count * nblk * width * width)
    lines = jnp.arange(width, dtype=jnp.int32)
    mask_on = (lines[None, :, None] < dims[:, 0][:, None, None]) & (
        lines[None, None, :] < dims[:, 1][:, None, None]
    )
    mask = mask_on.astype(jnp.float32)
    vzero = jnp.where(mask_on, start, jnp.zeros_like(start))
    hzero = apply_ham(vzero, lenv, renv, mask, offsets, device, nblk)
    vzero_f = vzero.astype(jnp.float32)
    nzero_part = jnp.sum(vzero_f * vzero_f)
    pzero_part = jnp.sum(vzero_f * hzero)
    nzero, pzero = lax.psum((nzero_part, pzero_part), "blk")
    scale = jnp.sqrt(cells / nzero)
    uzero = vzero_f * scale
    huzero = hzero * scale
    a_zero = pzero / nzero
    resid = huzero - a_zero * uzero
    squares = lax.psum(jnp.sum(resid * resid), "blk") / cells
    beta = jnp.sqrt(squares + 1e-06)
    vone = (resid / beta).astype(jnp.bfloat16)
    hone = apply_ham(vone, lenv, renv, mask, offsets, device, nblk)
    a_one = lax.psum(jnp.sum(vone.astype(jnp.float32) * hone), "blk") / cells
    half_gap = (a_zero - a_one) / 2.0
    ritz = (a_zero + a_one) / 2.0 - jnp.sqrt(half_gap * half_gap + beta * beta)
    gap_val = ritz - a_zero
    length = jnp.sqrt(beta * beta + gap_val * gap_val)
    xcoef = beta / length
    ycoef = gap_val / length
    state_new = (xcoef * uzero + ycoef * vone.astype(jnp.float32)).astype(jnp.bfloat16)
    hstate_new = (xcoef * huzero + ycoef * hone).astype(jnp.bfloat16)
    kept_on = lines[None, None, :] < kept_cols[:, None, None]
    kept = jnp.where(kept_on, state_new, jnp.zeros_like(state_new))
    kept_src = route_blocks(kept, offsets, device, nblk)
    pieces = []
    for ctype in range(5):
        inner = jnp.einsum(
            "wtab,tbc->wtac", lenv[ctype::5], kept_src[ctype], preferred_element_type=jnp.float32
        ).astype(jnp.bfloat16)
        piece = jnp.einsum(
            "tba,wtbc->wtac", kept, inner, preferred_element_type=jnp.float32
        ).astype(jnp.bfloat16)
        pieces.append(piece)
    stacked = jnp.stack(pieces, axis=1).reshape((channels, count, width, width))
    received = passed_along(stacked, "sec", 1)
    first_section = lax.axis_index("sec") == 0
    next_left = jnp.where(first_section, lenv, received)
    return (state_new[None], hstate_new[None], jnp.reshape(ritz, (1,)), next_left[None])


def solution(mesh):
    placed = (
        P("sec", "blk", None, None),
        P("sec", None, "blk", None, None),
        P("sec", None, "blk", None, None),
        P("sec", None),
        P("sec", "blk", None),
        P("sec", "blk"),
    )
    return jax.shard_map(
        shards,
        mesh=mesh,
        in_specs=placed,
        out_specs=(
            P("sec", "blk", None, None),
            P("sec", "blk", None, None),
            P("sec"),
            P("sec", None, "blk", None, None),
        ),
        check_vma=False,
    )
```

profile of v0, /device:TPU:1, one launch (start us, length us, event | category | flops | bytes accessed | tf_op | source)
XLA Modules:
  0.0 537.8 jit_solution(6096695522838150606)
XLA Ops:
  7.2 0.0 all-gather.4.cloned.1.call-start
  7.2 0.8 slice_bitcast_fusion.3
  8.0 0.1 iota_compare_fusion.1
  8.0 2.0 and_select_fusion
  10.1 0.0 all-gather.4.cloned.1.call-update
  10.1 0.0 all-gather.6.cloned.1.call-start
  10.3 1.3 fusion.370
  11.6 0.7 broadcast_compare_fusion
  12.2 0.8 slice_bitcast_fusion
  13.0 1.4 compare_and_fusion.2
  14.4 0.0 copy-start.2
  14.5 11.6 %copy_bitcast_fusion = (bf16[20,12,128,128]{3,2,0,1:T(8,128)(2,1)}, bf16[20,12,128,128]{3,2,0,1:T(8,128)(2,1)}) fusion(bf16[1,20,12,128,128]{4,3,2,1,0:T(8,128)(2,1)} %param.10, bf16[1,20,12,128,128]{4,3,2,1,0:T(8,128)(2,1)} %param.9), kind=kLoop, calls=%fused_computation.12 | loop fusion | bytes 31457280 | tf_op jit(solution)/shard_map/squeeze | solution.py:54
  26.0 0.0 copy-done.2
  26.0 2.9 fusion.45
  28.9 46.0 %all-gather.4.cloned.1.call-done = bf16[192,128,128]{2,1,0:T(8,128)(2,1)} async-done(((bf16[12,128,128]{2,1,0:T(8,128)(2,1)}), bf16[192,128,128]{2,1,0:T(8,128)(2,1)}) %all-gather.4.cloned.1.call-update) | async-done | bytes 6291472 | tf_op jit(solution)/shard_map/all_gather | solution.py:20
  74.9 3.4 gather_fusion
  78.3 3.4 fusion.140
  81.7 3.4 gather_fusion.1
  85.1 4.3 fusion.135
  89.4 3.4 gather_fusion.2
  92.8 0.0 copy-start
  92.8 3.6 fusion.130
  96.5 0.0 copy-start.4
  96.5 3.4 gather_fusion.3
  99.9 3.9 fusion.181
  103.8 31.8 %all-reduce = (f32[]{:T(128)}, f32[]{:T(128)}) all-reduce(f32[]{:T(128)} %get-tuple-element.10, f32[]{:T(128)} %get-tuple-element.9), channel_id=1, replica_groups=mesh['sec'=8,'blk'=16] {'blk'}, use_global_device_ids=true, to_apply=%region_3.5 | all-reduce | flops 2 | bytes 16 | tf_op jit(solution)/shard_map/psum | solution.py:74
  137.7 0.9 multiply_reduce_fusion
  138.6 29.1 %psum.30 = f32[]{:T(128)} all-reduce(f32[]{:T(128)} %multiply_reduce_fusion), channel_id=1, replica_groups=mesh['sec'=8,'blk'=16] {'blk'}, use_global_device_ids=true, to_apply=%region_5.7 | all-reduce | flops 1 | bytes 8 | tf_op jit(solution)/shard_map/psum | solution.py:80
  168.4 1.1 divide_convert_fusion
  169.5 0.0 all-gather.6.cloned.1.call-update
  169.5 0.2 all-gather.8.cloned.1.call-start
  169.8 0.1 iota_compare_fusion
  169.9 3.0 fusion.70
  172.9 70.0 %all-gather.6.cloned.1.call-done = bf16[192,128,128]{2,1,0:T(8,128)(2,1)} async-done(((bf16[12,128,128]{2,1,0:T(8,128)(2,1)}), bf16[192,128,128]{2,1,0:T(8,128)(2,1)}) %all-gather.6.cloned.1.call-update) | async-done | bytes 6291472 | tf_op jit(solution)/shard_map/all_gather | solution.py:20
  242.9 3.4 gather_fusion.4
  246.3 4.3 fusion.115
  250.6 3.4 gather_fusion.5
  254.0 0.0 copy-start.1
  254.0 3.6 fusion.110
  257.7 3.4 gather_fusion.6
  261.1 4.3 fusion.105
  265.4 3.4 gather_fusion.7
  268.8 4.1 fusion.180
  272.9 32.0 %psum.31 = f32[]{:T(128)} all-reduce(f32[]{:T(128)} %get-tuple-element.29), channel_id=1, replica_groups=mesh['sec'=8,'blk'=16] {'blk'}, use_global_device_ids=true, to_apply=%region_7.9 | all-reduce | flops 1 | bytes 8 | tf_op jit(solution)/shard_map/psum | solution.py:84
  305.7 1.1 broadcast_select_fusion
  306.8 0.0 all-gather.8.cloned.1.call-update
  306.9 3.8 bitcast_dynamic-update-slice_fusion.4
  310.7 61.1 %all-gather.8.cloned.1.call-done = bf16[192,128,128]{2,1,0:T(8,128)(2,1)} async-done(((bf16[12,128,128]{2,1,0:T(8,128)(2,1)}), bf16[192,128,128]{2,1,0:T(8,128)(2,1)}) %all-gather.8.cloned.1.call-update) | async-done | bytes 6291472 | tf_op jit(solution)/shard_map/all_gather | solution.py:20
  371.8 3.4 gather_fusion.8
  375.2 4.0 bitcast_dynamic-update-slice_fusion.3
  379.2 3.4 gather_fusion.9
  382.6 3.9 bitcast_dynamic-update-slice_fusion.2
  386.5 3.4 gather_fusion.10
  390.0 3.9 bitcast_dynamic-update-slice_fusion.1
  393.9 3.4 gather_fusion.11
  397.3 3.9 bitcast_dynamic-update-slice_fusion
  401.2 10.7 %copy.40 = bf16[4,5,12,128,128]{4,3,2,1,0:T(8,128)(2,1)} copy(bf16[4,5,12,128,128]{3,4,0,2,1:T(8,128)(2,1)} %bitcast_dynamic-update-slice_fusion) | data formatting | bytes 15728640 | tf_op jit(solution)/shard_map/stack | solution.py:105
  411.9 9.9 %copy.41 = bf16[20,12,128,128]{3,2,0,1:T(8,128)(2,1)} copy(bf16[20,12,128,128]{3,2,1,0:T(8,128)(2,1)} %bitcast.313) | data formatting | bytes 15728640 | tf_op jit(solution)/shard_map/reshape | solution.py:105
  421.8 3.9 collective-permute-start
  425.7 1.1 fusion.314
  426.8 0.9 fusion.183
  427.7 83.1 %collective-permute-done = bf16[20,12,128,128]{3,2,0,1:T(8,128)(2,1)} collective-permute-done((bf16[20,12,128,128]{3,2,0,1:T(8,128)(2,1)}, bf16[20,12,128,128]{3,2,0,1:T(8,128)(2,1)}, u32[]{:S(2)}, u32[]{:S(2)}) %collective-permute-start) | collective-permute-done | bytes 7864352 | tf_op jit(solution)/shard_map/ppermute | solution.py:10
  510.8 9.4 %select_bitcast_fusion = bf16[1,20,12,128,128]{4,3,1,2,0:T(8,128)(2,1)} fusion(bf16[20,12,128,128]{3,2,0,1:T(8,128)(2,1)} %collective-permute-done, pred[]{:T(512)S(6)} %eq.20, bf16[1,20,12,128,128]{4,3,2,1,0:T(8,128)(2,1)} %param.9), kind=kLoop, calls=%fused_computation.14 | loop fusion | flops 3932160 | bytes 23592960 | tf_op jit(solution)/shard_map/broadcast_in_dim | solution.py:109
  520.2 9.9 %copy.42 = bf16[1,20,12,128,128]{4,3,2,1,0:T(8,128)(2,1)} copy(bf16[1,20,12,128,128]{4,3,1,2,0:T(8,128)(2,1)} %select_bitcast_fusion) | data formatting | bytes 15728640
  (13 shorter events, 0.1 us)
Async XLA Ops:
  7.2 67.7 %all-gather.4.cloned.1.call-start = ((), (), s32[]{:S(2)}) async-start(), calls=%async_computation | async-start | bytes 6684672 | tf_op jit(solution)/shard_map/all_gather | solution.py:20
  10.1 232.8 %all-gather.6.cloned.1.call-start = ((), (), s32[]{:S(2)}) async-start(), calls=%async_computation.1 | async-start | bytes 6684672 | tf_op jit(solution)/shard_map/all_gather | solution.py:20
  14.4 11.6 %copy-start.2 = (bf16[12,128,128]{2,1,0:T(8,128)(2,1)S(1)}, bf16[12,128,128]{2,1,0:T(8,128)(2,1)}, u32[]{:S(2)}) copy-start(bf16[12,128,128]{2,1,0:T(8,128)(2,1)} %and_select_fusion) | copy-start | bytes 1179652
  92.8 44.9 %copy-start = (bf16[1,12,128,128]{3,2,1,0:T(8,128)(2,1)S(1)}, bf16[1,12,128,128]{3,2,1,0:T(8,128)(2,1)}, u32[]{:S(2)}) copy-start(bf16[1,12,128,128]{3,2,1,0:T(8,128)(2,1)} %param.8) | copy-start | bytes 1179652
  96.5 73.3 %copy-start.4 = (s32[1,12]{1,0:T(1,128)S(1)}, s32[1,12]{1,0:T(1,128)}, u32[]{:S(2)}) copy-start(s32[1,12]{1,0:T(1,128)} %param.13) | copy-start | bytes 148
  169.5 202.3 %all-gather.8.cloned.1.call-start = ((), (), s32[]{:S(2)}) async-start(), calls=%async_computation.2 | async-start | bytes 6684672 | tf_op jit(solution)/shard_map/all_gather | solution.py:20
  254.0 14.8 %copy-start.1 = (bf16[12,128,128]{2,1,0:T(8,128)(2,1)S(1)}, bf16[12,128,128]{2,1,0:T(8,128)(2,1)}, u32[]{:S(2)}) copy-start(bf16[12,128,128]{2,1,0:T(8,128)(2,1)} %divide_convert_fusion) | copy-start | bytes 1179652
  306.8 75.8 %copy-start.3 = (bf16[12,128,128]{2,1,0:T(8,128)(2,1)S(1)}, bf16[12,128,128]{2,1,0:T(8,128)(2,1)}, u32[]{:S(2)}) copy-start(bf16[12,128,128]{2,1,0:T(8,128)(2,1)} %broadcast_select_fusion) | copy-start | bytes 1179652
  421.8 89.0 %collective-permute-start = (bf16[20,12,128,128]{3,2,0,1:T(8,128)(2,1)}, bf16[20,12,128,128]{3,2,0,1:T(8,128)(2,1)}, u32[]{:S(2)}, u32[]{:S(2)}) collective-permute-start(bf16[20,12,128,128]{3,2,0,1:T(8,128)(2,1)} %copy.41), channel_id=1, source_target_pairs={{0,16},{16,32},{32,48},{48,64},{64,80},{80,96},{96,112},{1,17},{17... | collective-permute-start | bytes 23592968 | tf_op jit(solution)/shard_map/ppermute | solution.py:10
Sparse Core Ops, SparseCore 0:
  10.7 64.1 all-gather.3
  169.7 73.1 all-gather.5
  307.0 64.7 all-gather.7
where the time goes:
time: 539 us; the launch traced here: 538 us
  waiting for transfers between devices  260 us (48%)
  blocking collectives  92.9 us (17%)
  local copies, waits for them, and re-layouts  85.8 us (16%)
  matrix products  57.1 us (11%)
  other arithmetic  18.8 us (3%)
  between operations  18.8 us (3%)
    all_gather x3, waiting for transfers between devices, route_blocks(): whole = lax.all_gather(state, 'blk', axis=0, tiled=True)  177 us
    ppermute x1, waiting for transfers between devices, passed_along(): return lax.ppermute(value, axis, pairs)  83.1 us
    gather x12, local copies, waits for them, and re-layouts, route_blocks(): picked = [jnp.take(whole, entry, axis=0) for entry in indices]  40.9 us
    dot_general x10, matrix products, apply_ham(): jnp.einsum('wtac,wtdc->tad', inner, renv[ctype::5], preferred_element_typ...  37.5 us
    psum x1, blocking collectives, shards(): a_one = lax.psum(jnp.sum(vone.astype(jnp.float32) * hone), 'blk') / cells  32 us
    psum x1, blocking collectives, shards(): nzero, pzero = lax.psum((nzero_part, pzero_part), 'blk')  31.8 us
    psum x1, blocking collectives, shards(): squares = lax.psum(jnp.sum(resid * resid), 'blk') / cells  29.1 us
    dot_general x5, matrix products, shards(): jnp.einsum('tba,wtbc->wtac', kept, inner, preferred_element_type=jnp.floa...  19.6 us
  transfers between devices with their start and end apart: 4, of which 4 were waited for; matrix products, arithmetic and copies ran while one was open for 5% of the time, Pallas kernels for 0%

commit v1 on v0

--- a/solution.py
+++ b/solution.py
@@ -17,7 +17,9 @@
     next_off = jnp.roll(offsets, -1)
     down_val = (device - offsets) % nblk
     exists = [up_val >= 1, up_val <= count - 2, down_val >= 1, down_val <= nblk - 2]
-    whole = lax.all_gather(state, "blk", axis=0, tiled=True)
+    whole = jnp.concatenate(
+        lax.all_to_all(jnp.stack([state] * lax.axis_size("blk")), "blk", 0, 0), axis=0
+    )
     row_lo = jnp.clip(up_val - 1, 0, count - 1)
     row_hi = jnp.clip(up_val + 1, 0, count - 1)
     indices = [

time: 539 us -> 588 us (1.091)
  starting transfers between devices: 4.2 us -> 47.8 us
  between operations: 18.8 us -> 5.51 us
  waiting for transfers between devices: 260 us -> 271 us
    all_to_all x0 -> x3, waiting for transfers between devices: none -> 188 us  [route_blocks(): lax.all_to_all(jnp.stack([state] * lax.axis_size('blk')), 'blk', 0, 0)]
    all_gather x3 -> x0, waiting for transfers between devices: 177 us -> none  [route_blocks(): whole = lax.all_gather(state, 'blk', axis=0, tiled=True)]
    ppermute x1, starting transfers between devices: 3.9 us -> 30.4 us  [passed_along(): return lax.ppermute(value, axis, pairs)]
    all_to_all x0 -> x3, starting transfers between devices: none -> 17.4 us  [route_blocks(): lax.all_to_all(jnp.stack([state] * lax.axis_size('blk')), 'blk', 0, 0)]
    another operation x0 -> x3, local copies, waits for them, and re-layouts: none -> 12.7 us  [route_blocks(): jnp.stack([state] * lax.axis_size('blk'))]
    squeeze x1 -> x0, local copies, waits for them, and re-layouts: 11.6 us -> none  [shards(): renv = right_env[0]]
    reshape x1 -> x0, local copies, waits for them, and re-layouts: 9.9 us -> none  [shards(): stacked = jnp.stack(pieces, axis=1).reshape((channels, count, width, width))]
    gather x12, local copies, waits for them, and re-layouts: 40.9 us -> 49.9 us  [route_blocks(): picked = [jnp.take(whole, entry, axis=0) for entry in indices]]
  transfers between devices with their start and end apart: 4 -> 4, of which waited for: 4 -> 4; matrix products, arithmetic and copies ran while one was open for 5% -> 6% of each run, Pallas kernels for 0% -> 0%
where the time goes in v1:
time: 588 us; the launch traced here: 587 us
  waiting for transfers between devices  271 us (46%)
  blocking collectives  92.9 us (16%)
  local copies, waits for them, and re-layouts  89.9 us (15%)
  matrix products  59.3 us (10%)
  starting transfers between devices  47.8 us (8%)
  other arithmetic  19.8 us (3%)
    all_to_all x3, waiting for transfers between devices, route_blocks(): lax.all_to_all(jnp.stack([state] * lax.axis_size('blk')), 'blk', 0, 0)  188 us
    ppermute x1, waiting for transfers between devices, passed_along(): return lax.ppermute(value, axis, pairs)  83.1 us
    gather x12, local copies, waits for them, and re-layouts, route_blocks(): picked = [jnp.take(whole, entry, axis=0) for entry in indices]  49.9 us
    dot_general x10, matrix products, apply_ham(): jnp.einsum('wtac,wtdc->tad', inner, renv[ctype::5], preferred_element_typ...  40.1 us
    psum x1, blocking collectives, shards(): a_one = lax.psum(jnp.sum(vone.astype(jnp.float32) * hone), 'blk') / cells  32.1 us
    psum x1, blocking collectives, shards(): nzero, pzero = lax.psum((nzero_part, pzero_part), 'blk')  31.7 us
    ppermute x1, starting transfers between devices, passed_along(): return lax.ppermute(value, axis, pairs)  30.4 us
    psum x1, blocking collectives, shards(): squares = lax.psum(jnp.sum(resid * resid), 'blk') / cells  29.1 us
  transfers between devices with their start and end apart: 4, of which 4 were waited for; matrix products, arithmetic and copies ran while one was open for 6% of the time, Pallas kernels for 0%

profile of v1, /device:TPU:1, one launch (start us, length us, event | category | flops | bytes accessed | tf_op | source)
XLA Modules:
  0.0 586.6 jit_solution(7495068717136789051)
XLA Ops:
  0.6 0.8 slice_bitcast_fusion.3
  1.4 0.1 iota_compare_fusion.1
  1.5 1.3 fusion.183
  2.7 4.2 stack.21
  7.0 7.6 %all-to-all-start = ((bf16[16,12,128,128]{3,2,1,0:T(8,128)(2,1)}), bf16[16,12,128,128]{3,2,1,0:T(8,128)(2,1)}, u32[]{:S(2)}, u32[]{:S(2)}) async-start(bf16[16,12,128,128]{3,2,1,0:T(8,128)(2,1)} %stack.21), calls=%async_computation | async-start | bytes 12582912 | tf_op jit(solution)/shard_map/all_to_all | solution.py:21
  14.6 0.0 copy-start.3
  14.6 9.9 %copy.93 = bf16[1,20,12,128,128]{4,3,1,2,0:T(8,128)(2,1)} copy(bf16[1,20,12,128,128]{4,3,2,1,0:T(8,128)(2,1)} %param.10) | data formatting | bytes 15728640 | tf_op args[2]
  24.6 0.5 iota_compare_fusion.4
  25.1 0.5 iota_compare_fusion.3
  25.6 0.5 compare_and_fusion.1
  26.1 0.6 compare_and_fusion
  26.7 0.6 fusion.372
  27.3 0.6 broadcast_compare_fusion
  27.8 0.1 slice_bitcast_fusion
  27.9 2.0 compare_and_fusion.2
  29.9 0.6 pad_clamp_fusion
  30.5 5.2 fusion.371
  35.7 4.4 fusion.45
  40.1 66.9 %all-to-all-done = bf16[16,12,128,128]{3,2,1,0:T(8,128)(2,1)} async-done(((bf16[16,12,128,128]{3,2,1,0:T(8,128)(2,1)}), bf16[16,12,128,128]{3,2,1,0:T(8,128)(2,1)}, u32[]{:S(2)}, u32[]{:S(2)}) %all-to-all-start) | async-done | bytes 6291488 | tf_op jit(solution)/shard_map/all_to_all | solution.py:21
  107.1 4.1 gather_fusion
  111.2 4.1 gather_fusion.1
  115.3 4.3 gather_fusion.2
  119.6 4.3 gather_fusion.3
  123.9 4.1 fusion.140
  128.0 4.1 fusion.135
  132.2 3.7 fusion.130
  135.8 3.4 fusion.181
  139.3 31.7 %all-reduce = (f32[]{:T(128)}, f32[]{:T(128)}) all-reduce(f32[]{:T(128)} %get-tuple-element.6, f32[]{:T(128)} %get-tuple-element.5), channel_id=1, replica_groups=mesh['sec'=8,'blk'=16] {'blk'}, use_global_device_ids=true, to_apply=%region_3.5 | all-reduce | flops 2 | bytes 16 | tf_op jit(solution)/shard_map/psum | solution.py:76
  173.1 0.9 multiply_reduce_fusion
  174.0 29.1 %psum.30 = f32[]{:T(128)} all-reduce(f32[]{:T(128)} %multiply_reduce_fusion), channel_id=1, replica_groups=mesh['sec'=8,'blk'=16] {'blk'}, use_global_device_ids=true, to_apply=%region_5.7 | all-reduce | flops 1 | bytes 8 | tf_op jit(solution)/shard_map/psum | solution.py:82
  203.8 0.3 divide_convert_fusion
  204.1 4.2 stack.22
  208.4 4.9 all-to-all-start.1
  213.3 0.1 iota_compare_fusion
  213.4 3.7 fusion.70
  217.2 65.2 %all-to-all-done.1 = bf16[16,12,128,128]{3,2,1,0:T(8,128)(2,1)} async-done(((bf16[16,12,128,128]{3,2,1,0:T(8,128)(2,1)}), bf16[16,12,128,128]{3,2,1,0:T(8,128)(2,1)}, u32[]{:S(2)}, u32[]{:S(2)}) %all-to-all-start.1) | async-done | bytes 6291488 | tf_op jit(solution)/shard_map/all_to_all | solution.py:21
  282.4 4.3 gather_fusion.4
  286.6 4.1 gather_fusion.5
  290.8 4.3 gather_fusion.6
  295.0 3.5 gather_fusion.7
  298.6 4.1 fusion.115
  302.7 4.1 fusion.110
  306.9 4.2 fusion.105
  311.0 4.1 fusion.180
  315.2 32.1 %psum.31 = f32[]{:T(128)} all-reduce(f32[]{:T(128)} %get-tuple-element.30), channel_id=1, replica_groups=mesh['sec'=8,'blk'=16] {'blk'}, use_global_device_ids=true, to_apply=%region_7.9 | all-reduce | flops 1 | bytes 8 | tf_op jit(solution)/shard_map/psum | solution.py:86
  348.1 0.3 broadcast_select_fusion
  348.4 4.2 stack.24
  352.7 4.9 all-to-all-start.2
  357.5 3.6 bitcast_dynamic-update-slice_fusion.4
  361.1 56.2 %all-to-all-done.2 = bf16[16,12,128,128]{3,2,1,0:T(8,128)(2,1)} async-done(((bf16[16,12,128,128]{3,2,1,0:T(8,128)(2,1)}), bf16[16,12,128,128]{3,2,1,0:T(8,128)(2,1)}, u32[]{:S(2)}, u32[]{:S(2)}) %all-to-all-start.2) | async-done | bytes 6291488 | tf_op jit(solution)/shard_map/all_to_all | solution.py:21
  417.3 4.3 gather_fusion.8
  421.6 4.1 gather_fusion.9
  425.7 4.3 gather_fusion.10
  430.0 4.3 gather_fusion.11
  434.3 4.0 bitcast_dynamic-update-slice_fusion.3
  438.3 4.0 bitcast_dynamic-update-slice_fusion.2
  442.3 4.0 bitcast_dynamic-update-slice_fusion.1
  446.4 3.5 bitcast_dynamic-update-slice_fusion
  449.9 10.7 %copy.12 = bf16[4,5,12,128,128]{4,3,2,1,0:T(8,128)(2,1)} copy(bf16[4,5,12,128,128]{3,4,0,2,1:T(8,128)(2,1)} %bitcast_dynamic-update-slice_fusion) | data formatting | bytes 15728640 | tf_op jit(solution)/shard_map/stack | solution.py:107
  460.5 30.4 %collective-permute-start = (bf16[20,12,128,128]{3,2,1,0:T(8,128)(2,1)}, bf16[20,12,128,128]{3,2,1,0:T(8,128)(2,1)}, u32[]{:S(2)}, u32[]{:S(2)}) collective-permute-start(bf16[20,12,128,128]{3,2,1,0:T(8,128)(2,1)} %bitcast.333), channel_id=1, source_target_pairs={{0,16},{16,32},{32,48},{48,64},{64,80},{80,96},{96,112},{1,17},{17... | collective-permute-start | bytes 23592968 | tf_op jit(solution)/shard_map/ppermute | solution.py:10
  490.9 1.1 fusion.315
  492.0 0.9 fusion.184
  492.9 83.1 %collective-permute-done = bf16[20,12,128,128]{3,2,1,0:T(8,128)(2,1)} collective-permute-done((bf16[20,12,128,128]{3,2,1,0:T(8,128)(2,1)}, bf16[20,12,128,128]{3,2,1,0:T(8,128)(2,1)}, u32[]{:S(2)}, u32[]{:S(2)}) %collective-permute-start) | collective-permute-done | bytes 7864352 | tf_op jit(solution)/shard_map/ppermute | solution.py:10
  576.0 9.5 %select_bitcast_fusion = bf16[1,20,12,128,128]{4,3,2,1,0:T(8,128)(2,1)} fusion(bf16[20,12,128,128]{3,2,1,0:T(8,128)(2,1)} %collective-permute-done, pred[]{:T(512)S(6)} %eq.20, bf16[1,20,12,128,128]{4,3,2,1,0:T(8,128)(2,1)} %param.9), kind=kLoop, calls=%fused_computation.13 | loop fusion | flops 3932160 | bytes 23592960 | tf_op jit(solution)/shard_map/broadcast_in_dim | solution.py:111
  (26 shorter events, 0.1 us)
Async XLA Ops:
  7.0 100.1 %all-to-all-start = ((bf16[16,12,128,128]{3,2,1,0:T(8,128)(2,1)}), bf16[16,12,128,128]{3,2,1,0:T(8,128)(2,1)}, u32[]{:S(2)}, u32[]{:S(2)}) async-start(bf16[16,12,128,128]{3,2,1,0:T(8,128)(2,1)} %stack.21), calls=%async_computation | async-start | bytes 12582912 | tf_op jit(solution)/shard_map/all_to_all | solution.py:21
  14.6 12.0 %copy-start.3 = (s32[1,12]{1,0:T(1,128)S(1)}, s32[1,12]{1,0:T(1,128)}, u32[]{:S(2)}) copy-start(s32[1,12]{1,0:T(1,128)} %param.11) | copy-start | bytes 148
  29.9 77.2 %copy-start.4 = (s32[1024]{0:T(1024)}, s32[1024]{0:T(1024)S(1)}, u32[]{:S(2)}) copy-start(s32[1024]{0:T(1024)S(1)} %get-tuple-element.35) | copy-start | bytes 12292
  30.5 5.2 copy-start
  35.7 96.4 %copy-start.1 = (bf16[4,12,128,128]{3,2,1,0:T(8,128)(2,1)}, bf16[4,12,128,128]{3,2,1,0:T(8,128)(2,1)S(1)}, u32[]{:S(2)}) copy-start(bf16[4,12,128,128]{3,2,1,0:T(8,128)(2,1)S(1)} %get-tuple-element.16) | copy-start | bytes 4718596
  111.2 12.7 %copy-start.9 = (pred[12]{0:T(512)(128)(4,1)S(1)}, pred[12]{0:T(512)(128)(4,1)}, u32[]{:S(2)}) copy-start(pred[12]{0:T(512)(128)(4,1)} %get-tuple-element.23) | copy-start | bytes 40
  128.0 4.1 copy-start.6
  208.4 5.0 copy-start.5
  208.4 74.0 %all-to-all-start.1 = ((bf16[16,12,128,128]{3,2,1,0:T(8,128)(2,1)}), bf16[16,12,128,128]{3,2,1,0:T(8,128)(2,1)}, u32[]{:S(2)}, u32[]{:S(2)}) async-start(bf16[16,12,128,128]{3,2,1,0:T(8,128)(2,1)} %stack.22), calls=%async_computation.1 | async-start | bytes 12582912 | tf_op jit(solution)/shard_map/all_to_all | solution.py:21
  352.7 64.7 %all-to-all-start.2 = ((bf16[16,12,128,128]{3,2,1,0:T(8,128)(2,1)}), bf16[16,12,128,128]{3,2,1,0:T(8,128)(2,1)}, u32[]{:S(2)}, u32[]{:S(2)}) async-start(bf16[16,12,128,128]{3,2,1,0:T(8,128)(2,1)} %stack.24), calls=%async_computation.2 | async-start | bytes 12582912 | tf_op jit(solution)/shard_map/all_to_all | solution.py:21
  417.3 16.9 %copy-start.10 = (pred[12]{0:T(512)(128)(4,1)S(1)}, pred[12]{0:T(512)(128)(4,1)}, u32[]{:S(2)}) copy-start(pred[12]{0:T(512)(128)(4,1)} %get-tuple-element.23) | copy-start | bytes 40
  434.3 4.0 copy-start.8
  438.3 4.0 copy-start.7
  442.3 4.0 copy-start.11
  460.5 31.5 %copy-start.2 = (f32[12,128,128]{2,1,0:T(8,128)S(1)}, f32[12,128,128]{2,1,0:T(8,128)}, u32[]{:S(2)}) copy-start(f32[12,128,128]{2,1,0:T(8,128)} %get-tuple-element.31) | copy-start | bytes 2359300
  460.5 115.4 %collective-permute-start = (bf16[20,12,128,128]{3,2,1,0:T(8,128)(2,1)}, bf16[20,12,128,128]{3,2,1,0:T(8,128)(2,1)}, u32[]{:S(2)}, u32[]{:S(2)}) collective-permute-start(bf16[20,12,128,128]{3,2,1,0:T(8,128)(2,1)} %bitcast.333), channel_id=1, source_target_pairs={{0,16},{16,32},{32,48},{48,64},{64,80},{80,96},{96,112},{1,17},{17... | collective-permute-start | bytes 23592968 | tf_op jit(solution)/shard_map/ppermute | solution.py:10
